TPU v7x, 256 devices: a whole 4x4x8 slice. The times are simulated.
256 devices in a mesh: dp: 2 (over core), width: 4 (over x), vocab: 32 (over z, y).
Axes of the slice: x: 4, y: 4, z: 8, core: 2. Of those that a mesh axis runs over, the one named last changes fastest.
Arguments:
- hidden: bfloat16 [1024, 8192], P('dp', 'width'), may hold values from -68 to 68
- head: bfloat16 [8192, 2, 32064], P('width', 'dp', 'vocab'), may hold values from -0.25 to 0.25
- teacher: bfloat16 [1024, 2, 32064], P('dp', None, 'vocab'), may hold values from -180 to 180
Outputs:
- divergence: float32 [1024], P('dp')
- grad_head: bfloat16 [8192, 2, 32064], P('width', 'dp', 'vocab')
- grad_hidden: bfloat16 [1024, 8192], P('dp', 'width')
All inputs are finite; a program needn't handle non-finite values.
Results may differ from a plain program's by a relative error of at most 0.0052.
Values may be sent and summed in bfloat16 or wider, within the bound.
A program may use at most 128 MiB of HBM per device.

v0:
```python
import jax
import jax.numpy as jnp
from jax import lax
from jax.sharding import PartitionSpec as P

VOCAB = 64128


def body(hidden, head, teacher):
    tok_rows, width_cols = hidden.shape
    halves = teacher.shape[1]
    local_cols = teacher.shape[2]
    full_head = lax.all_gather(head, "dp", axis=1, tiled=True).reshape(
        width_cols, halves * local_cols
    )
    partial_value = jnp.dot(hidden, full_head, preferred_element_type=jnp.float32)
    student = lax.psum(partial_value, "width")
    target = teacher.reshape(tok_rows, halves * local_cols).astype(jnp.float32)
    student_peak = jnp.max(student, axis=1)
    target_peak = jnp.max(target, axis=1)
    student_peak, target_peak = lax.pmax((student_peak, target_peak), "vocab")
    target_exp = jnp.exp(target - target_peak[:, None])
    student_total, target_total, cross_total = lax.psum(
        (
            jnp.sum(jnp.exp(student - student_peak[:, None]), axis=1),
            jnp.sum(target_exp, axis=1),
            jnp.sum(target_exp * (target - student), axis=1),
        ),
        "vocab",
    )
    student_lse = student_peak + jnp.log(student_total)
    target_lse = target_peak + jnp.log(target_total)
    divergence = cross_total / target_total - target_lse + student_lse
    prob_student = jnp.exp(student - student_lse[:, None])
    prob_target = jnp.exp(target - target_lse[:, None])
    grad = (VOCAB * (prob_student - prob_target)).astype(jnp.bfloat16)
    grad_blocks = grad.reshape(tok_rows, halves, local_cols)
    blocks = width_cols * lax.axis_size("dp") // width_cols
    term = jnp.einsum("td,tkv->kdv", hidden, grad_blocks, preferred_element_type=jnp.float32)
    head_term = lax.psum_scatter(
        term.reshape(blocks * width_cols, local_cols), "dp", scatter_dimension=0, tiled=True
    )
    grad_head = head_term.astype(jnp.bfloat16).reshape(width_cols, 1, local_cols)
    hidden_term = lax.dot_general(
        grad, full_head, (((1,), (1,)), ((), ())), preferred_element_type=jnp.float32
    )
    grad_hidden = lax.psum(hidden_term, "vocab").astype(jnp.bfloat16)
    return (divergence, grad_head, grad_hidden)


def solution(mesh):
    return jax.shard_map(
        body,
        mesh=mesh,
        in_specs=(P("dp", "width"), P("width", "dp", "vocab"), P("dp", None, "vocab")),
        out_specs=(P("dp"), P("width", "dp", "vocab"), P("dp", "width")),
        check_vma=False,
    )
```

profile of v0, /device:TPU:8, one launch (start us, length us, event | category | flops | bytes accessed | tf_op | source)
XLA Modules:
  0.0 544.9 jit_solution(12567613389792812008)
XLA Ops:
  7.2 0.0 copy-start
  7.2 0.0 all-gather.2.cloned.1.call-start
  7.2 0.7 all-gather.2.cloned.1.call-update
  7.9 0.0 all-reduce.6.cloned.1.call-start
  8.0 29.7 %all-gather.2.cloned.1.call-done = bf16[2048,2,1002]{0,2,1:T(8,128)(2,1)} async-done(((bf16[2048,1,1002]{0,2,1:T(8,128)(2,1)}), bf16[2048,2,1002]{0,2,1:T(8,128)(2,1)}) %all-gather.2.cloned.1.call-update) | async-done | bytes 8208400 | tf_op jit(solution)/shard_map/all_gather | solution.py:13
  37.7 8.1 %reshape.29 = bf16[2048,2004]{0,1:T(8,128)(2,1)} reshape(bf16[2048,2,1002]{0,2,1:T(8,128)(2,1)} %all-gather.2.cloned.1.call-done) | data formatting | bytes 16416768 | tf_op jit(solution)/shard_map/reshape | solution.py:13
  45.8 0.0 copy-done
  45.8 8.8 %fusion.1 = f32[512,2004]{0,1:T(8,128)} fusion(bf16[512,2048]{1,0:T(8,128)(2,1)S(1)} %copy-done, bf16[2048,2004]{0,1:T(8,128)(2,1)} %reshape.29), kind=kOutput, calls=%fused_computation.10 | convolution fusion | flops 4202692608 | bytes 14409728 | tf_op jit(solution)/shard_map/dot_general | solution.py:16
  54.6 0.0 all-reduce.6.cloned.1.call-update
  54.6 0.0 reduce-scatter.2.cloned.1.call-start
  54.7 4.2 copy.13
  58.8 3.3 reduce_max.23
  62.1 4.5 reshape.33
  66.7 86.0 %all-reduce.6.cloned.1.call-done = f32[512,2004]{0,1:T(8,128)} async-done(((f32[512,2004]{0,1:T(8,128)}), f32[512,2004]{0,1:T(8,128)}) %all-reduce.6.cloned.1.call-update) | async-done | bytes 4104208 | tf_op jit(solution)/shard_map/psum | solution.py:17
  152.7 2.5 reduce_max.25
  155.2 71.3 %all-reduce.2 = (f32[512]{0:T(512)S(1)}, f32[512]{0:T(512)S(1)}) all-reduce(f32[512]{0:T(512)S(1)} %reduce_max.25, bf16[512]{0:T(512)(128)(2,1)S(1)} %reduce_max.23), channel_id=1, replica_groups=mesh['dp'=2,'width'=4,'vocab'=32] {'vocab'}, use_global_device_ids=true, to_apply=%region_8.0 | all-reduce | flops 1024 | bytes 7168 | tf_op jit(solution)/shard_map/pmax | solution.py:21
  226.5 4.9 exponential_reduce_fusion.1
  231.4 4.8 multiply_reduce_fusion
  236.1 74.1 %all-reduce.1 = (f32[512]{0:T(512)S(1)}, f32[512]{0:T(512)S(1)}) all-reduce(f32[512]{0:T(512)S(1)} %get-tuple-element.13, f32[512]{0:T(512)S(1)} %exponential_reduce_fusion.1), channel_id=1, replica_groups=mesh['dp'=2,'width'=4,'vocab'=32] {'vocab'}, use_global_device_ids=true, to_apply=%region_10.0 | all-reduce | flops 1024 | bytes 8192 | tf_op jit(solution)/shard_map/psum | solution.py:23
  310.3 5.9 %multiply_convert_fusion = bf16[512,2004]{0,1:T(8,128)(2,1)} fusion(f32[512,2004]{0,1:T(8,128)} %reshape.33, f32[512,2004]{0,1:T(8,128)} %all-reduce.6.cloned.1.call-done, f32[512]{0:T(512)S(1)} %get-tuple-element.21, f32[512]{0:T(512)S(1)} %get-tuple-element.20), kind=kLoop, calls=%fused_computation.2 | loop fusion | flops 5130240 | bytes 10264576 | tf_op jit(solution)/shard_map/convert_element_type | solution.py:36
  316.2 3.3 reshape.30
  319.5 9.5 %convolution_bitcast_fusion = f32[2,2048,1002]{1,2,0:T(8,128)} fusion(bf16[512,2,1002]{0,2,1:T(8,128)(2,1)} %reshape.30, bf16[512,2048]{1,0:T(8,128)(2,1)S(1)} %copy-done), kind=kOutput, calls=%fused_computation | convolution fusion | flops 4202692608 | bytes 20566016 | tf_op jit(solution)/shard_map/td,tkv->kdv/dot_general | solution.py:39
  329.0 17.9 %copy.14 = f32[2,2048,1002]{2,1,0:T(8,128)} copy(f32[2,2048,1002]{1,2,0:T(8,128)} %convolution_bitcast_fusion) | data formatting | bytes 32833536 | tf_op jit(solution)/shard_map/td,tkv->kdv/transpose | solution.py:39
  346.9 0.0 copy-start.2
  346.9 0.0 reduce-scatter.2.cloned.1.call-update
  346.9 1.6 copy-done.2
  348.5 9.5 %fusion.2 = f32[512,2048]{1,0:T(8,128)} fusion(bf16[512,2004]{0,1:T(8,128)(2,1)S(1)} %copy-done.2, bf16[2048,2004]{0,1:T(8,128)(2,1)} %reshape.29), kind=kOutput, calls=%fused_computation.11 | convolution fusion | flops 4202692608 | bytes 14454784 | tf_op jit(solution)/shard_map/dot_general | solution.py:44
  358.0 167.2 %all-reduce.7 = (f32[512]{0:T(512)S(1)}, bf16[512,2048]{1,0:T(8,128)(2,1)}) all-reduce(f32[512]{0:T(512)S(1)} %get-tuple-element.12, f32[512,2048]{1,0:T(8,128)} %fusion.2), channel_id=1, replica_groups=mesh['dp'=2,'width'=4,'vocab'=32] {'vocab'}, use_global_device_ids=true, to_apply=%region_4.0 | all-reduce | flops 1049088 | bytes 6295552 | tf_op jit(solution)/shard_map/psum | solution.py:23
  525.2 0.6 subtract_add_fusion
  525.8 6.1 %convert_bitcast_fusion = bf16[2048,1,1002]{2,0,1:T(8,128)(2,1)} fusion(f32[2048,1002]{1,0:T(8,128)} %reduce-scatter.2.cloned.1.call-done), kind=kLoop, calls=%fused_computation.1 | loop fusion | flops 2052096 | bytes 12312576 | tf_op jit(solution)/shard_map/reshape | solution.py:43
  531.9 6.5 %copy.15 = bf16[2048,1,1002]{0,2,1:T(8,128)(2,1)} copy(bf16[2048,1,1002]{2,0,1:T(8,128)(2,1)} %convert_bitcast_fusion) | data formatting | bytes 8208384
  538.4 0.0 copy-done.1
  (3 shorter events, 0.0 us)
Async XLA Ops:
  7.2 38.6 %copy-start = (bf16[512,2048]{1,0:T(8,128)(2,1)S(1)}, bf16[512,2048]{1,0:T(8,128)(2,1)}, u32[]{:S(2)}) copy-start(bf16[512,2048]{1,0:T(8,128)(2,1)} %param.3) | copy-start | bytes 6291460
  7.2 30.5 %all-gather.2.cloned.1.call-start = ((), (), s32[]{:S(2)}) async-start(), calls=%async_computation.1 | async-start | bytes 12386304 | tf_op jit(solution)/shard_map/all_gather | solution.py:13
  7.9 144.8 %all-reduce.6.cloned.1.call-start = ((), (), s32[]{:S(2)}) async-start(), calls=%async_computation.2 | async-start | bytes 8224768 | tf_op jit(solution)/shard_map/psum | solution.py:17
  54.6 471.2 %reduce-scatter.2.cloned.1.call-start = ((), (), s32[]{:S(2)}) async-start(), calls=%async_computation.3 | async-start | bytes 25165824 | tf_op jit(solution)/shard_map/reduce_scatter | solution.py:40
  346.9 1.6 copy-start.2
  525.8 12.6 %copy-start.1 = (bf16[512,2048]{1,0:T(8,128)(2,1)S(1)}, bf16[512,2048]{1,0:T(8,128)(2,1)}, u32[]{:S(2)}) copy-start(bf16[512,2048]{1,0:T(8,128)(2,1)} %param.3) | copy-start | bytes 6291460
Sparse Core Ops, SparseCore 0:
  9.8 27.8 all-gather.1
  54.7 97.9 all-reduce.5
  347.0 26.0 reduce-scatter.1
where the time goes:
time: 549 us; the launch traced here: 545 us
  blocking collectives  313 us (57%)
  waiting for transfers between devices  116 us (21%)
  local copies, waits for them, and re-layouts  46 us (8%)
  other arithmetic  28.1 us (5%)
  matrix products  27.8 us (5%)
  between operations  13.8 us (3%)
    psum x2, blocking collectives, body(): lax.psum((jnp.sum(jnp.exp(student - student_peak[:, None]), axis=1), jnp....  241 us
    psum x1, waiting for transfers between devices, body(): student = lax.psum(partial_value, 'width')  86 us
    pmax x1, blocking collectives, body(): student_peak, target_peak = lax.pmax((student_peak, target_peak), 'vocab')  71.3 us
    all_gather x1, waiting for transfers between devices, body(): lax.all_gather(head, 'dp', axis=1, tiled=True)  29.7 us
    transpose x1, local copies, waits for them, and re-layouts, body(): jnp.einsum('td,tkv->kdv', hidden, grad_blocks, preferred_element_type=jnp...  17.9 us
  transfers between devices with their start and end apart: 3, of which 2 were waited for; matrix products, arithmetic and copies ran while one was open for 4% of the time, Pallas kernels for 0%

commit v1 on v0

v1 whole, which is shorter than its diff:
```python
import jax
import jax.numpy as jnp
from jax import lax
from jax.experimental import pallas as pl
from jax.experimental.pallas import tpu as pltpu
from jax.sharding import PartitionSpec as P

VOCAB = 64128
MESH = pl.DeviceIdType.MESH
BF16, F32 = jnp.bfloat16, jnp.float32
WIRE = F32
NEG = -1e30
K = 2
ROWS, REAL, BULK = 1008, 1002, 1000
BLK = 128
PAIR = 2 * BLK
CHUNK = 2 * PAIR
WID = 2048
HALF = 512
TOK4 = PAIR // 4
COL8 = WID // 8

HID, TEA, STAT1, STAT2, PAIRSUM, ZSUM, ZOUT = range(7)
XRS, XAG, YRS, YAG = 7, 13, 17, 23
DIV = 27
NSEM = 28
LHID, LTEA, LOUT = range(3)


class Ring4:
    def __init__(self, axis, pos, device, send, recv):
        self.p = pos
        self.right = device(lax.rem(pos + 1, 4))
        self.left = device(lax.rem(pos + 3, 4))
        self.send, self.recv = send, recv

    def copy(self, src, dst, n, k, peer):
        return pltpu.make_async_remote_copy(
            src_ref=src, dst_ref=dst, send_sem=self.send.at[k, n], recv_sem=self.recv.at[k, n],
            device_id=peer, device_id_type=MESH,
        )


class ReduceScatter4(Ring4):
    def setup(self, k, base, src, first, second, half):
        p = self.p
        nxt, opp, prv = lax.rem(p + 1, 4), lax.rem(p + 2, 4), lax.rem(p + 3, 4)
        rows = src.shape[2]
        a, b = pl.ds(0, half), pl.ds(half, rows - half)
        self.c1 = [
            self.copy(src.at[k, opp, a], first.at[k, 0, a], base + 0, k, self.right),
            self.copy(src.at[k, opp, b], first.at[k, 1, pl.ds(0, rows - half)], base + 1, k, self.left),
        ]
        self.c2 = [
            self.copy(src.at[k, nxt, b], second.at[k, 0, b], base + 2, k, self.right),
            self.copy(src.at[k, prv, a], second.at[k, 1, a], base + 3, k, self.left),
        ]
        self.c3 = [
            self.copy(first.at[k, 0, a], second.at[k, 0, a], base + 4, k, self.right),
            self.copy(first.at[k, 1, pl.ds(0, rows - half)], second.at[k, 1, b], base + 5, k, self.left),
        ]
        self.args = (k, src, first, half, rows, nxt, prv)
        return self

    def start1(self):
        for c in self.c1:
            c.start()

    def start2(self):
        for c in self.c2:
            c.start()

    def relay(self):
        k, src, first, half, rows, nxt, prv = self.args
        self.c1[0].wait_recv()
        s = first[k, 0, 0:half].astype(F32) + src[k, nxt, 0:half].astype(F32)
        first[k, 0, 0:half] = s.astype(first.dtype)
        self.c3[0].start()
        self.c1[1].wait_recv()
        s = first[k, 1, 0 : rows - half].astype(F32) + src[k, prv, half:rows].astype(F32)
        first[k, 1, 0 : rows - half] = s.astype(first.dtype)
        self.c3[1].start()

    def finish(self):
        for c in self.c2 + self.c3:
            c.wait_recv()

    def drain(self):
        for c in self.c1 + self.c2 + self.c3:
            c.wait_send()


class AllGather4(Ring4):
    def setup(self, k, base, buf, half):
        p = self.p
        nxt, prv = lax.rem(p + 1, 4), lax.rem(p + 3, 4)
        rows = buf.shape[2]
        a, b = pl.ds(0, half), pl.ds(half, rows - half)
        self.c1 = [
            self.copy(buf.at[k, p], buf.at[k, p], base + 0, k, self.right),
            self.copy(buf.at[k, p], buf.at[k, p], base + 1, k, self.left),
        ]
        self.c2 = [
            self.copy(buf.at[k, prv, a], buf.at[k, prv, a], base + 2, k, self.right),
            self.copy(buf.at[k, nxt, b], buf.at[k, nxt, b], base + 3, k, self.left),
        ]
        return self

    def start1(self):
        for c in self.c1:
            c.start()

    def relay(self):
        self.c1[0].wait_recv()
        self.c2[0].start()
        self.c1[1].wait_recv()
        self.c2[1].start()

    def finish(self):
        for c in self.c2:
            c.wait_recv()

    def drain(self):
        for c in self.c1 + self.c2:
            c.wait_send()


def merge(tiles):
    ms = [t[0:1] for t in tiles]
    mt = [t[2:3] for t in tiles]
    top_s, top_t = ms[0], mt[0]
    for i in range(1, len(tiles)):
        top_s, top_t = jnp.maximum(top_s, ms[i]), jnp.maximum(top_t, mt[i])
    sum_s = sum_t = cross = jnp.zeros_like(top_s)
    for t, a, b in zip(tiles, ms, mt):
        fs, ft = jnp.exp(a - top_s), jnp.exp(b - top_t)
        sum_s = sum_s + t[1:2] * fs
        sum_t = sum_t + t[3:4] * ft
        cross = cross + t[4:5] * ft
    return top_s, sum_s, top_t, sum_t, cross


def kernel(
    hid_ref, head_ref, tail_ref, tea_ref, div_ref, gh_ref, ghid_ref,
    hid, head, tea, part, first, second, logit, st0, st1, st2, st3, grad, gradn,
    theirs, arrive, mine, ysrc, yfirst, ysecond, zsrc, zin, fin, gout, divs,
    send, recv, local, head_sem, out_sem,
):
    c = lax.axis_index("dp")
    w = lax.axis_index("width")
    v = lax.axis_index("vocab")
    y, z = lax.rem(v, 4), v // 4
    partner = {"dp": 1 - c}

    def x_dev(q):
        return {"width": q}

    def y_dev(q):
        return {"vocab": z * 4 + q}

    def cy(i):
        j = lax.rem(c * 4 + y + i, 8)
        return {"dp": j // 4, "vocab": z * 4 + lax.rem(j, 4)}

    def z_dev(i):
        return {"vocab": lax.rem(z + i, 8) * 4 + y}

    head_copies = [
        pltpu.make_async_copy(head_ref.at[pl.ds(0, BULK)], head.at[pl.ds(0, BULK)], head_sem.at[0]),
        pltpu.make_async_copy(tail_ref, head.at[pl.ds(BULK, ROWS - BULK)], head_sem.at[1]),
    ]
    for cp in head_copies:
        cp.start()
    hid_copies = [
        pltpu.make_async_copy(hid_ref.at[pl.ds(k * PAIR, PAIR)], hid.at[k, c], local.at[k, LHID]) for k in range(K)
    ]
    for cp in hid_copies:
        cp.start()

    barrier = pltpu.get_barrier_semaphore()
    for i in range(1, 8):
        pl.semaphore_signal(barrier, inc=1, device_id=cy(i), device_id_type=MESH)
        pl.semaphore_signal(barrier, inc=1, device_id=z_dev(i), device_id_type=MESH)
    for i in range(1, 4):
        pl.semaphore_signal(barrier, inc=1, device_id=x_dev(lax.rem(w + i, 4)), device_id_type=MESH)
    pl.semaphore_wait(barrier, 17)

    def remote(src, dst, n, k, peer):
        return pltpu.make_async_remote_copy(
            src_ref=src, dst_ref=dst, send_sem=send.at[k, n], recv_sem=recv.at[k, n],
            device_id=peer, device_id_type=MESH,
        )

    hid_sends = [remote(hid_ref.at[pl.ds(k * PAIR, PAIR)], hid.at[k, c], HID, k, partner) for k in range(K)]
    for cp in hid_sends:
        cp.start()
    holder = c == w // 2
    place = lax.rem(w, 2) * BLK

    def tea_copy(k):
        cols = pl.ds(pl.multiple_of(k * PAIR + place, BLK), BLK)
        return (
            pltpu.make_async_copy(tea_ref.at[c, :, cols], tea.at[k], local.at[k, LTEA]),
            remote(tea_ref.at[1 - c, :, cols], tea.at[k], TEA, k, partner),
        )

    tea_copies = [tea_copy(k) for k in range(K)]

    @pl.when(holder)
    def _():
        for here, there in tea_copies:
            there.start()
            here.start()

    xrs = [ReduceScatter4("width", w, x_dev, send, recv).setup(k, XRS, part, first, second, HALF) for k in range(K)]
    xag = [AllGather4("width", w, x_dev, send, recv).setup(k, XAG, grad, HALF) for k in range(K)]
    yrs = [
        ReduceScatter4("vocab", y, y_dev, send, recv).setup(k, YRS, ysrc, yfirst, ysecond, TOK4 // 2) for k in range(K)
    ]
    yag = [AllGather4("vocab", y, y_dev, send, recv).setup(k, YAG, fin, TOK4 // 2) for k in range(K)]

    def logits(k, d):
        for lo, hi in ((0, HALF), (HALF, ROWS)):
            out = lax.dot_general(
                head[lo:hi, :], hid[k, d], (((1,), (1,)), ((), ())), preferred_element_type=F32
            )
            part[k, 2 * d, lo:hi] = out[:, :BLK].astype(WIRE)
            part[k, 2 * d + 1, lo:hi] = out[:, BLK:].astype(WIRE)

    def wait_hidden(k):
        hid_copies[k].wait()
        hid_sends[k].wait_recv()

    def statistics(k):
        xrs[k].finish()

        @pl.when(holder)
        def _():
            tea_copies[k][0].wait()

        @pl.when(jnp.logical_not(holder))
        def _():
            tea_copies[k][1].wait_recv()

        x = part[k, w].astype(F32) + second[k, 0].astype(F32) + second[k, 1].astype(F32)
        row = lax.broadcasted_iota(jnp.int32, x.shape, 0)
        x = jnp.where(row < REAL, x, NEG)
        logit[k] = x
        t = tea[k].astype(F32)
        top_s = jnp.max(x, axis=0, keepdims=True)
        top_t = jnp.max(t, axis=0, keepdims=True)
        exp_t = jnp.exp(t - top_t)
        st0[k, 0:1] = top_s
        st0[k, 1:2] = jnp.sum(jnp.exp(x - top_s), axis=0, keepdims=True)
        st0[k, 2:3] = top_t
        st0[k, 3:4] = jnp.sum(exp_t, axis=0, keepdims=True)
        st0[k, 4:5] = jnp.sum(exp_t * (t - x), axis=0, keepdims=True)
        st0[k, 5:8] = jnp.zeros((3, BLK), F32)
        me = c * 4 + y
        st1[k, me] = st0[k]
        for i in range(1, 8):
            remote(st0.at[k], st1.at[k, me], STAT1, k, cy(i)).start()

    def seven(buf, k):
        return buf.at[k, pl.ds(0, 7)]

    def statistics_far(k):
        remote(seven(st1, k), seven(st1, k), STAT1, k, cy(1)).wait_recv()
        got = merge([st1[k, i] for i in range(8)])
        for i in range(5):
            st2[k, i : i + 1] = got[i]
        st2[k, 5:8] = jnp.zeros((3, BLK), F32)
        st3[k, z] = st2[k]
        for i in range(1, 8):
            remote(st2.at[k], st3.at[k, z], STAT2, k, z_dev(i)).start()

    def gradient(k):
        remote(seven(st3, k), seven(st3, k), STAT2, k, z_dev(1)).wait_recv()
        top_s, sum_s, top_t, sum_t, cross = merge([st3[k, i] for i in range(8)])
        lse_s = top_s + jnp.log(sum_s)
        lse_t = top_t + jnp.log(sum_t)
        divs[k, w] = jnp.broadcast_to(cross / sum_t - lse_t + lse_s, (8, BLK))
        g = VOCAB * (jnp.exp(logit[k] - lse_s) - jnp.exp(tea[k].astype(F32) - lse_t))
        grad[k, w] = g.astype(BF16)
        xag[k].start1()
        for i in range(1, 4):
            remote(divs.at[k, w], divs.at[k, w], DIV, k, x_dev(lax.rem(w + i, 4))).start()

    def hidden_terms(k):
        xag[k].finish()
        for d, final in ((1 - c, False), (c, True)):
            gn = jnp.concatenate([grad[k, 2 * d], grad[k, 2 * d + 1]], axis=1)
            gradn[...] = gn.T

            def tile(j, carry):
                cols = pl.ds(pl.multiple_of(j * 512, 512), 512)
                out = jnp.dot(gradn[...], head[:, cols], preferred_element_type=F32)
                if final:
                    mine[:, cols] = out
                else:
                    theirs[k, :, cols] = out.astype(BF16)
                return carry

            lax.fori_loop(0, WID // 512, tile, 0)
            if not final:
                remote(theirs.at[k], arrive.at[k], PAIRSUM, k, partner).start()

    def pair_sum(k):
        remote(theirs.at[k], arrive.at[k], PAIRSUM, k, partner).wait_recv()
        for i in range(4):
            rows = slice(i * TOK4, (i + 1) * TOK4)
            ysrc[k, i] = (mine[rows] + arrive[k, rows].astype(F32)).astype(BF16)
        yrs[k].start1()
        yrs[k].start2()

    def z_sum(k):
        yrs[k].finish()
        s = ysrc[k, y].astype(F32) + ysecond[k, 0].astype(F32) + ysecond[k, 1].astype(F32)
        s = s.astype(BF16)
        for i in range(8):
            zsrc[k, i] = s[:, i * COL8 : (i + 1) * COL8]
        zin[k, z] = zsrc[k, z]
        for i in range(1, 8):
            q = lax.rem(z + i, 8)
            remote(zsrc.at[k, q], zin.at[k, z], ZSUM, k, z_dev(i)).start()

    def my_cols():
        return pl.ds(pl.multiple_of(z * COL8, COL8), COL8)

    def z_gather(k):
        remote(seven(zin, k), seven(zin, k), ZSUM, k, z_dev(1)).wait_recv()
        s = zin[k, 0].astype(F32)
        for i in range(1, 8):
            s = s + zin[k, i].astype(F32)
        fin[k, y, :, my_cols()] = s.astype(BF16)
        mine_ref = fin.at[k, y, :, my_cols()]
        for i in range(1, 8):
            remote(mine_ref, mine_ref, ZOUT, k, z_dev(i)).start()

    def y_gather(k):
        span = fin.at[k, y, :, pl.ds(0, 7 * COL8)]
        remote(span, span, ZOUT, k, z_dev(1)).wait_recv()
        yag[k].start1()

    def put_hidden(k):
        yag[k].finish()
        for i in range(4):
            pltpu.make_async_copy(
                fin.at[k, i], ghid_ref.at[pl.ds(k * PAIR + i * TOK4, TOK4)], out_sem.at[k, i]
            ).start()

    def head_terms(js):
        for j in js:
            cols = slice(j * 256, (j + 1) * 256)
            for lo, hi in ((0, HALF), (HALF, ROWS)):
                total = None
                for k in range(K):
                    g = jnp.concatenate([grad[k, b, lo:hi] for b in range(4)], axis=1)
                    h = hid[k, :, :, cols].reshape(CHUNK, 256)
                    term = jnp.dot(g, h, preferred_element_type=F32)
                    total = term if total is None else total + term
                gout[lo:hi, cols] = total.astype(BF16)
            pltpu.make_async_copy(gout.at[:, cols], gh_ref.at[:, cols], out_sem.at[2, j]).start()

    for cp in head_copies[:0]:
        cp.wait()
    opp, own = 1 - w // 2, w // 2
    wait_hidden(0)
    for cp in head_copies:
        cp.wait()
    logits(0, opp)
    xrs[0].start1()
    logits(0, own)
    xrs[0].start2()
    wait_hidden(1)
    logits(1, opp)
    logits(1, own)
    xrs[0].relay()
    xrs[1].start1()
    xrs[1].start2()
    statistics(0)
    xrs[1].relay()
    statistics_far(0)
    gradient(0)
    statistics(1)
    xag[0].relay()
    statistics_far(1)
    hidden_terms(0)
    gradient(1)
    pair_sum(0)
    xag[1].relay()
    yrs[0].relay()
    z_sum(0)
    hidden_terms(1)
    z_gather(0)
    pair_sum(1)
    y_gather(0)
    head_terms((0, 1))
    yrs[1].relay()
    yag[0].relay()
    head_terms((2,))
    z_sum(1)
    put_hidden(0)
    head_terms((3, 4))
    z_gather(1)
    head_terms((5,))
    y_gather(1)
    head_terms((6, 7))
    yag[1].relay()
    for k in range(K):
        span3 = divs.at[k, pl.ds(0, 3)]
        remote(span3, span3, DIV, k, x_dev(lax.rem(w + 1, 4))).wait_recv()
        for i in range(2):
            div_ref[2 * k + i : 2 * k + i + 1] = divs[k, 2 * c + i, 0:1]
    put_hidden(1)

    for k in range(K):
        hid_sends[k].wait_send()
        for r in (xrs[k], xag[k], yrs[k], yag[k]):
            r.drain()
        remote(seven(st1, k), seven(st1, k), STAT1, k, cy(1)).wait_send()
        remote(seven(st3, k), seven(st3, k), STAT2, k, z_dev(1)).wait_send()
        remote(theirs.at[k], arrive.at[k], PAIRSUM, k, partner).wait_send()
        remote(seven(zin, k), seven(zin, k), ZSUM, k, z_dev(1)).wait_send()
        span = fin.at[k, y, :, pl.ds(0, 7 * COL8)]
        remote(span, span, ZOUT, k, z_dev(1)).wait_send()
        span3 = divs.at[k, pl.ds(0, 3)]
        remote(span3, span3, DIV, k, x_dev(lax.rem(w + 1, 4))).wait_send()
        for i in range(4):
            pltpu.make_async_copy(
                fin.at[k, i], ghid_ref.at[pl.ds(k * PAIR + i * TOK4, TOK4)], out_sem.at[k, i]
            ).wait()
    for j in range(8):
        cols = slice(j * 256, (j + 1) * 256)
        pltpu.make_async_copy(gout.at[:, cols], gh_ref.at[:, cols], out_sem.at[2, j]).wait()

    @pl.when(holder)
    def _():
        for _, there in tea_copies:
            there.wait_send()


def body(hidden, head, teacher):
    head_t = head.reshape(WID, REAL).T
    tail = jnp.pad(head_t[BULK:], ((0, ROWS - REAL), (0, 0)))
    teacher_t = jnp.pad(
        jnp.transpose(teacher, (1, 2, 0)), ((0, 0), (0, ROWS - REAL), (0, 0)), constant_values=NEG
    )
    any_space = pl.BlockSpec(memory_space=pl.ANY)
    vmem = pltpu.VMEM
    div, gh, ghid = pl.pallas_call(
        kernel,
        out_shape=(
            jax.ShapeDtypeStruct((4, BLK), F32),
            jax.ShapeDtypeStruct((ROWS, WID), BF16),
            jax.ShapeDtypeStruct((K * PAIR, WID), BF16),
        ),
        in_specs=[any_space] * 4,
        out_specs=(pl.BlockSpec(memory_space=pltpu.VMEM), any_space, any_space),
        scratch_shapes=[
            vmem((K, 2, PAIR, WID), BF16),
            vmem((ROWS, WID), BF16),
            vmem((K, ROWS, BLK), BF16),
            vmem((K, 4, ROWS, BLK), WIRE),
            vmem((K, 2, HALF, BLK), WIRE),
            vmem((K, 2, ROWS, BLK), WIRE),
            vmem((K, ROWS, BLK), F32),
            vmem((K, 8, BLK), F32),
            vmem((K, 8, 8, BLK), F32),
            vmem((K, 8, BLK), F32),
            vmem((K, 8, 8, BLK), F32),
            vmem((K, 4, ROWS, BLK), BF16),
            vmem((PAIR, ROWS), BF16),
            vmem((K, PAIR, WID), BF16),
            vmem((K, PAIR, WID), BF16),
            vmem((PAIR, WID), F32),
            vmem((K, 4, TOK4, WID), BF16),
            vmem((K, 2, TOK4 // 2, WID), BF16),
            vmem((K, 2, TOK4, WID), BF16),
            vmem((K, 8, TOK4, COL8), BF16),
            vmem((K, 8, TOK4, COL8), BF16),
            vmem((K, 4, TOK4, WID), BF16),
            vmem((ROWS, WID), BF16),
            vmem((K, 4, 8, BLK), F32),
            pltpu.SemaphoreType.DMA((K, NSEM)),
            pltpu.SemaphoreType.DMA((K, NSEM)),
            pltpu.SemaphoreType.DMA((K, 2)),
            pltpu.SemaphoreType.DMA((2,)),
            pltpu.SemaphoreType.DMA((3, 8)),
        ],
        compiler_params=pltpu.CompilerParams(
            collective_id=0, has_side_effects=True, vmem_limit_bytes=60 * 1024 * 1024
        ),
    )(hidden, head_t, tail, teacher_t)
    return div.reshape(K * PAIR), gh[:REAL].T.reshape(WID, 1, REAL), ghid


def solution(mesh):
    return jax.shard_map(
        body,
        mesh=mesh,
        in_specs=(P("dp", "width"), P("width", "dp", "vocab"), P("dp", None, "vocab")),
        out_specs=(P("dp"), P("width", "dp", "vocab"), P("dp", "width")),
        check_vma=False,
    )
```

time: 549 us -> 141 us (0.26)
  blocking collectives: 313 us -> 0 us
  Pallas kernels: 0 us -> 128 us
  waiting for transfers between devices: 116 us -> 0 us
  local copies, waits for them, and re-layouts: 46 us -> 11.5 us
  other arithmetic: 28.1 us -> 0 us
  matrix products: 27.8 us -> 0 us
  between operations: 13.8 us -> 0.66 us
    psum x2 -> x0, blocking collectives: 241 us -> none  [body(): lax.psum((jnp.sum(jnp.exp(student - student_peak[:, None]), axis=1), jnp....]
    pallas_call x0 -> x1, Pallas kernels: none -> 128 us  [body(): pl.pallas_call(kernel, out_shape=(jax.ShapeDtypeStruct((4, BLK), F32), ja...]
    psum x1 -> x0, waiting for transfers between devices: 86 us -> none  [body(): student = lax.psum(partial_value, 'width')]
    pmax x1 -> x0, blocking collectives: 71.3 us -> none  [body(): student_peak, target_peak = lax.pmax((student_peak, target_peak), 'vocab')]
    all_gather x1 -> x0, waiting for transfers between devices: 29.7 us -> none  [body(): lax.all_gather(head, 'dp', axis=1, tiled=True)]
    dot_general x3 -> x0, matrix products: 27.8 us -> none  [the longest x1 9.53 us: body(): lax.dot_general(grad, full_head, (((1,), (1,)), ((), ())), preferred_elem...]
    transpose x1 -> x0, local copies, waits for them, and re-layouts: 17.9 us -> none  [body(): jnp.einsum('td,tkv->kdv', hidden, grad_blocks, preferred_element_type=jnp...]
    reduce_sum x2 -> x0, other arithmetic: 9.63 us -> none  [the longest x1 4.86 us: body(): jnp.sum(target_exp, axis=1)]
  transfers between devices with their start and end apart: 3 -> 0, of which waited for: 2 -> 0; matrix products, arithmetic and copies ran while one was open for 4% -> 0% of each run, Pallas kernels for 0% -> 0%
where the time goes in v1:
time: 141 us; the launch traced here: 140 us
  Pallas kernels  128 us (91%)
  local copies, waits for them, and re-layouts  11.5 us (8%)
    pallas_call x1, Pallas kernels, body(): pl.pallas_call(kernel, out_shape=(jax.ShapeDtypeStruct((4, BLK), F32), ja...  128 us
    reshape x1, local copies, waits for them, and re-layouts, body(): return (div.reshape(K * PAIR), gh[:REAL].T.reshape(WID, 1, REAL), ghid)  4.88 us
    unnamed x7, local copies, waits for them, and re-layouts  3.81 us

profile of v1, /device:TPU:8, one launch (start us, length us, event | category | flops | bytes accessed | tf_op | source)
XLA Modules:
  0.0 140.2 jit_solution(7854436402967914930)
XLA Ops:
  0.6 0.8 slice.8
  1.4 0.6 pad.8.tail_ref
  2.0 1.9 %copy.8 = bf16[512,2,1002]{0,2,1:T(8,128)(2,1)S(1)} copy(bf16[512,2,1002]{0,1,2:T(2,128)(2,1)} %param.5) | data formatting | bytes 4104192 | tf_op args[2]
  3.9 1.4 %pad.9.tea_ref = bf16[2,1008,512]{2,1,0:T(8,128)(2,1)} pad(bf16[2,1002,512]{2,1,0:T(8,128)(2,1)S(1)} %bitcast.11, bf16[]{:T(256)} %constant.5.clone.1), padding=0_0x0_6x0_0 | pad | bytes 4116482 | tf_op jit(solution)/shard_map/jit(_pad)/pad | solution.py:446
  5.4 128.0 %shard_map.58 = (f32[4,128]{1,0:T(4,128)}, bf16[1008,2048]{1,0:T(8,128)(2,1)}, bf16[512,2048]{1,0:T(8,128)(2,1)}) custom-call(bf16[512,2048]{1,0:T(8,128)(2,1)} %hid_ref.1, bf16[1002,2048]{1,0:T(8,128)(2,1)} %bitcast.13, bf16[8,2048]{1,0:T(8,128)(2,1)} %pad.8.tail_ref, bf16[2,1008,512]{2,1,0:T(8,128)(2,1)} %pad.9.tea_ref), custom_call_target="tpu_custom_call" | custom-call | tf_op jit(solution)/shard_map/pallas_call | solution.py:451
  133.4 0.0 copy-start.1
  133.4 0.0 copy-start
  133.4 4.9 %slice_bitcast_fusion = bf16[2048,1,1002]{0,2,1:T(8,128)(2,1)} fusion(bf16[1008,2048]{1,0:T(8,128)(2,1)} %get-tuple-element.7), kind=kLoop, calls=%fused_computation | loop fusion | bytes 8208384 | tf_op jit(solution)/shard_map/reshape | solution.py:495
  138.3 0.0 copy-done.1
  138.3 0.6 copy.11
  138.9 0.0 copy-done
  138.9 1.3 copy.12
Async XLA Ops:
  133.4 4.9 %copy-start.1 = (f32[4,128]{1,0:T(4,128)S(1)}, f32[4,128]{1,0:T(4,128)}, u32[]{:S(2)}) copy-start(f32[4,128]{1,0:T(4,128)} %get-tuple-element.6) | copy-start | bytes 6148
  133.4 5.5 %copy-start = (bf16[512,2048]{1,0:T(8,128)(2,1)S(1)}, bf16[512,2048]{1,0:T(8,128)(2,1)}, u32[]{:S(2)}) copy-start(bf16[512,2048]{1,0:T(8,128)(2,1)} %get-tuple-element.14) | copy-start | bytes 6291460

commit v2 on v1

--- a/solution.py
+++ b/solution.py
@@ -9,9 +9,8 @@
 MESH = pl.DeviceIdType.MESH
 BF16, F32 = jnp.bfloat16, jnp.float32
 WIRE = F32
-NEG = -1e30
 K = 2
-ROWS, REAL, BULK = 1008, 1002, 1000
+ROWS, REAL = 1008, 1002
 BLK = 128
 PAIR = 2 * BLK
 CHUNK = 2 * PAIR
@@ -141,7 +140,7 @@
 
 
 def kernel(
-    hid_ref, head_ref, tail_ref, tea_ref, div_ref, gh_ref, ghid_ref,
+    hid_ref, head_ref, tea_ref, div_ref, gh_ref, ghid_ref,
     hid, head, tea, part, first, second, logit, st0, st1, st2, st3, grad, gradn,
     theirs, arrive, mine, ysrc, yfirst, ysecond, zsrc, zin, fin, gout, divs,
     send, recv, local, head_sem, out_sem,
@@ -165,12 +164,8 @@
     def z_dev(i):
         return {"vocab": lax.rem(z + i, 8) * 4 + y}
 
-    head_copies = [
-        pltpu.make_async_copy(head_ref.at[pl.ds(0, BULK)], head.at[pl.ds(0, BULK)], head_sem.at[0]),
-        pltpu.make_async_copy(tail_ref, head.at[pl.ds(BULK, ROWS - BULK)], head_sem.at[1]),
-    ]
-    for cp in head_copies:
-        cp.start()
+    head_copy = pltpu.make_async_copy(head_ref, head, head_sem.at[0])
+    head_copy.start()
     hid_copies = [
         pltpu.make_async_copy(hid_ref.at[pl.ds(k * PAIR, PAIR)], hid.at[k, c], local.at[k, LHID]) for k in range(K)
     ]
@@ -220,7 +215,10 @@
     yag = [AllGather4("vocab", y, y_dev, send, recv).setup(k, YAG, fin, TOK4 // 2) for k in range(K)]
 
     def logits(k, d):
-        for lo, hi in ((0, HALF), (HALF, ROWS)):
+        for lo, hi in ((0, HALF), (HALF, REAL)):
+            if hi == REAL:
+                part[k, 2 * d, ROWS - 8 : ROWS] = jnp.zeros((8, BLK), WIRE)
+                part[k, 2 * d + 1, ROWS - 8 : ROWS] = jnp.zeros((8, BLK), WIRE)
             out = lax.dot_general(
                 head[lo:hi, :], hid[k, d], (((1,), (1,)), ((), ())), preferred_element_type=F32
             )
@@ -242,9 +240,7 @@
         def _():
             tea_copies[k][1].wait_recv()
 
-        x = part[k, w].astype(F32) + second[k, 0].astype(F32) + second[k, 1].astype(F32)
-        row = lax.broadcasted_iota(jnp.int32, x.shape, 0)
-        x = jnp.where(row < REAL, x, NEG)
+        x = part[k, w, 0:REAL] + second[k, 0, 0:REAL] + second[k, 1, 0:REAL]
         logit[k] = x
         t = tea[k].astype(F32)
         top_s = jnp.max(x, axis=0, keepdims=True)
@@ -281,7 +277,8 @@
         lse_t = top_t + jnp.log(sum_t)
         divs[k, w] = jnp.broadcast_to(cross / sum_t - lse_t + lse_s, (8, BLK))
         g = VOCAB * (jnp.exp(logit[k] - lse_s) - jnp.exp(tea[k].astype(F32) - lse_t))
-        grad[k, w] = g.astype(BF16)
+        grad[k, w, ROWS - 16 : ROWS] = jnp.zeros((16, BLK), BF16)
+        grad[k, w, 0:REAL] = g.astype(BF16)
         xag[k].start1()
         for i in range(1, 4):
             remote(divs.at[k, w], divs.at[k, w], DIV, k, x_dev(lax.rem(w + i, 4))).start()
@@ -294,7 +291,7 @@
 
             def tile(j, carry):
                 cols = pl.ds(pl.multiple_of(j * 512, 512), 512)
-                out = jnp.dot(gradn[...], head[:, cols], preferred_element_type=F32)
+                out = jnp.dot(gradn[:, 0:REAL], head[:, cols], preferred_element_type=F32)
                 if final:
                     mine[:, cols] = out
                 else:
@@ -352,7 +349,7 @@
     def head_terms(js):
         for j in js:
             cols = slice(j * 256, (j + 1) * 256)
-            for lo, hi in ((0, HALF), (HALF, ROWS)):
+            for lo, hi in ((0, HALF), (HALF, REAL)):
                 total = None
                 for k in range(K):
                     g = jnp.concatenate([grad[k, b, lo:hi] for b in range(4)], axis=1)
@@ -362,12 +359,9 @@
                 gout[lo:hi, cols] = total.astype(BF16)
             pltpu.make_async_copy(gout.at[:, cols], gh_ref.at[:, cols], out_sem.at[2, j]).start()
 
-    for cp in head_copies[:0]:
-        cp.wait()
     opp, own = 1 - w // 2, w // 2
     wait_hidden(0)
-    for cp in head_copies:
-        cp.wait()
+    head_copy.wait()
     logits(0, opp)
     xrs[0].start1()
     logits(0, own)
@@ -442,29 +436,26 @@
 
 def body(hidden, head, teacher):
     head_t = head.reshape(WID, REAL).T
-    tail = jnp.pad(head_t[BULK:], ((0, ROWS - REAL), (0, 0)))
-    teacher_t = jnp.pad(
-        jnp.transpose(teacher, (1, 2, 0)), ((0, 0), (0, ROWS - REAL), (0, 0)), constant_values=NEG
-    )
+    teacher_t = jnp.transpose(teacher, (1, 2, 0))
     any_space = pl.BlockSpec(memory_space=pl.ANY)
     vmem = pltpu.VMEM
     div, gh, ghid = pl.pallas_call(
         kernel,
         out_shape=(
             jax.ShapeDtypeStruct((4, BLK), F32),
-            jax.ShapeDtypeStruct((ROWS, WID), BF16),
+            jax.ShapeDtypeStruct((REAL, WID), BF16),
             jax.ShapeDtypeStruct((K * PAIR, WID), BF16),
         ),
-        in_specs=[any_space] * 4,
+        in_specs=[any_space] * 3,
         out_specs=(pl.BlockSpec(memory_space=pltpu.VMEM), any_space, any_space),
         scratch_shapes=[
             vmem((K, 2, PAIR, WID), BF16),
-            vmem((ROWS, WID), BF16),
-            vmem((K, ROWS, BLK), BF16),
+            vmem((REAL, WID), BF16),
+            vmem((K, REAL, BLK), BF16),
             vmem((K, 4, ROWS, BLK), WIRE),
             vmem((K, 2, HALF, BLK), WIRE),
             vmem((K, 2, ROWS, BLK), WIRE),
-            vmem((K, ROWS, BLK), F32),
+            vmem((K, REAL, BLK), F32),
             vmem((K, 8, BLK), F32),
             vmem((K, 8, 8, BLK), F32),
             vmem((K, 8, BLK), F32),
@@ -480,19 +471,19 @@
             vmem((K, 8, TOK4, COL8), BF16),
             vmem((K, 8, TOK4, COL8), BF16),
             vmem((K, 4, TOK4, WID), BF16),
-            vmem((ROWS, WID), BF16),
+            vmem((REAL, WID), BF16),
             vmem((K, 4, 8, BLK), F32),
             pltpu.SemaphoreType.DMA((K, NSEM)),
             pltpu.SemaphoreType.DMA((K, NSEM)),
             pltpu.SemaphoreType.DMA((K, 2)),
-            pltpu.SemaphoreType.DMA((2,)),
+            pltpu.SemaphoreType.DMA((1,)),
             pltpu.SemaphoreType.DMA((3, 8)),
         ],
         compiler_params=pltpu.CompilerParams(
             collective_id=0, has_side_effects=True, vmem_limit_bytes=60 * 1024 * 1024
         ),
-    )(hidden, head_t, tail, teacher_t)
-    return div.reshape(K * PAIR), gh[:REAL].T.reshape(WID, 1, REAL), ghid
+    )(hidden, head_t, teacher_t)
+    return div.reshape(K * PAIR), gh.T.reshape(WID, 1, REAL), ghid
 
 
 def solution(mesh):

time: 141 us -> 139 us (0.986)
    unnamed x7 -> x6, local copies, waits for them, and re-layouts: 3.81 us -> 10.7 us
    reshape x1 -> x0, local copies, waits for them, and re-layouts: 4.88 us -> none  [body(): return (div.reshape(K * PAIR), gh[:REAL].T.reshape(WID, 1, REAL), ghid)]
    pad x2 -> x0, local copies, waits for them, and re-layouts: 2.07 us -> none  [the longest x1 1.44 us: body(): jnp.pad(jnp.transpose(teacher, (1, 2, 0)), ((0, 0), (0, ROWS - REAL), (0,...]
where the time goes in v2:
time: 139 us
  Pallas kernels  128 us (92%)
  local copies, waits for them, and re-layouts  10.7 us (8%)
    pallas_call x1, Pallas kernels, body(): pl.pallas_call(kernel, out_shape=(jax.ShapeDtypeStruct((4, BLK), F32), ja...  128 us
    unnamed x6, local copies, waits for them, and re-layouts  10.7 us

profile of v2, /device:TPU:8, one launch (start us, length us, event | category | flops | bytes accessed | tf_op | source)
XLA Modules:
  0.0 139.3 jit_solution(10410002993548424990)
XLA Ops:
  0.6 3.2 %copy.8 = bf16[512,2,1002]{0,2,1:T(8,128)(2,1)} copy(bf16[512,2,1002]{0,1,2:T(2,128)(2,1)} %param.5) | data formatting | bytes 4104192 | tf_op args[2]
  3.8 128.0 %shard_map.58 = (f32[4,128]{1,0:T(4,128)}, bf16[1002,2048]{1,0:T(8,128)(2,1)}, bf16[512,2048]{1,0:T(8,128)(2,1)}) custom-call(bf16[512,2048]{1,0:T(8,128)(2,1)} %hid_ref.1, bf16[1002,2048]{1,0:T(8,128)(2,1)} %bitcast.11, bf16[2,1002,512]{2,1,0:T(8,128)(2,1)} %bitcast.10), custom_call_target="tpu_custom_call" | custom-call | tf_op jit(solution)/shard_map/pallas_call | solution.py:442
  131.9 1.3 copy.12
  133.1 0.0 copy-start
  133.1 4.9 %copy.13 = bf16[2048,1,1002]{0,2,1:T(8,128)(2,1)} copy(bf16[2048,1,1002]{0,2,1:T(8,128)(2,1)} %bitcast.12) | data formatting | bytes 8208384
  138.0 0.0 copy-done
  138.0 1.3 copy.14
Async XLA Ops:
  133.1 4.9 %copy-start = (bf16[512,2048]{1,0:T(8,128)(2,1)S(1)}, bf16[512,2048]{1,0:T(8,128)(2,1)}, u32[]{:S(2)}) copy-start(bf16[512,2048]{1,0:T(8,128)(2,1)} %get-tuple-element.14) | copy-start | bytes 6291460

commit v3 on v2

--- a/solution.py
+++ b/solution.py
@@ -17,7 +17,9 @@
 WID = 2048
 HALF = 512
 TOK4 = PAIR // 4
-COL8 = WID // 8
+PARTS = 2 * K
+WID2 = WID // 2
+COL8 = WID2 // 8
 
 HID, TEA, STAT1, STAT2, PAIRSUM, ZSUM, ZOUT = range(7)
 XRS, XAG, YRS, YAG = 7, 13, 17, 23
@@ -210,9 +212,9 @@
     xrs = [ReduceScatter4("width", w, x_dev, send, recv).setup(k, XRS, part, first, second, HALF) for k in range(K)]
     xag = [AllGather4("width", w, x_dev, send, recv).setup(k, XAG, grad, HALF) for k in range(K)]
     yrs = [
-        ReduceScatter4("vocab", y, y_dev, send, recv).setup(k, YRS, ysrc, yfirst, ysecond, TOK4 // 2) for k in range(K)
+        ReduceScatter4("vocab", y, y_dev, send, recv).setup(k, YRS, ysrc, yfirst, ysecond, TOK4 // 2) for k in range(PARTS)
     ]
-    yag = [AllGather4("vocab", y, y_dev, send, recv).setup(k, YAG, fin, TOK4 // 2) for k in range(K)]
+    yag = [AllGather4("vocab", y, y_dev, send, recv).setup(k, YAG, fin, TOK4 // 2) for k in range(PARTS)]
 
     def logits(k, d):
         for lo, hi in ((0, HALF), (HALF, REAL)):
@@ -289,26 +291,33 @@
             gn = jnp.concatenate([grad[k, 2 * d], grad[k, 2 * d + 1]], axis=1)
             gradn[...] = gn.T
 
-            def tile(j, carry):
-                cols = pl.ds(pl.multiple_of(j * 512, 512), 512)
-                out = jnp.dot(gradn[:, 0:REAL], head[:, cols], preferred_element_type=F32)
-                if final:
-                    mine[:, cols] = out
-                else:
-                    theirs[k, :, cols] = out.astype(BF16)
-                return carry
-
-            lax.fori_loop(0, WID // 512, tile, 0)
-            if not final:
-                remote(theirs.at[k], arrive.at[k], PAIRSUM, k, partner).start()
+            for half in range(2):
+                n = 2 * k + half
+
+                def tile(j, carry):
+                    here = pl.ds(pl.multiple_of(j * 512, 512), 512)
+                    cols = pl.ds(pl.multiple_of(half * WID2 + j * 512, 512), 512)
+                    out = jnp.dot(gradn[:, 0:REAL], head[:, cols], preferred_element_type=F32)
+                    if final:
+                        mine[:, cols] = out
+                    else:
+                        theirs[n, :, here] = out.astype(BF16)
+                    return carry
+
+                lax.fori_loop(0, WID2 // 512, tile, 0)
+                if not final:
+                    remote(theirs.at[n], arrive.at[n], PAIRSUM, n, partner).start()
 
     def pair_sum(k):
-        remote(theirs.at[k], arrive.at[k], PAIRSUM, k, partner).wait_recv()
-        for i in range(4):
-            rows = slice(i * TOK4, (i + 1) * TOK4)
-            ysrc[k, i] = (mine[rows] + arrive[k, rows].astype(F32)).astype(BF16)
-        yrs[k].start1()
-        yrs[k].start2()
+        for half in range(2):
+            n = 2 * k + half
+            remote(theirs.at[n], arrive.at[n], PAIRSUM, n, partner).wait_recv()
+            cols = slice(half * WID2, (half + 1) * WID2)
+            for i in range(4):
+                rows = slice(i * TOK4, (i + 1) * TOK4)
+                ysrc[n, i] = (mine[rows, cols] + arrive[n, rows].astype(F32)).astype(BF16)
+            yrs[n].start1()
+            yrs[n].start2()
 
     def z_sum(k):
         yrs[k].finish()
@@ -339,12 +348,15 @@
         remote(span, span, ZOUT, k, z_dev(1)).wait_recv()
         yag[k].start1()
 
-    def put_hidden(k):
-        yag[k].finish()
+    def out_copy(n, i):
+        rows = pl.ds(n // 2 * PAIR + i * TOK4, TOK4)
+        cols = pl.ds(n % 2 * WID2, WID2)
+        return pltpu.make_async_copy(fin.at[n, i], ghid_ref.at[rows, cols], out_sem.at[n, i])
+
+    def put_hidden(n):
+        yag[n].finish()
         for i in range(4):
-            pltpu.make_async_copy(
-                fin.at[k, i], ghid_ref.at[pl.ds(k * PAIR + i * TOK4, TOK4)], out_sem.at[k, i]
-            ).start()
+            out_copy(n, i).start()
 
     def head_terms(js):
         for j in js:
@@ -357,7 +369,7 @@
                     term = jnp.dot(g, h, preferred_element_type=F32)
                     total = term if total is None else total + term
                 gout[lo:hi, cols] = total.astype(BF16)
-            pltpu.make_async_copy(gout.at[:, cols], gh_ref.at[:, cols], out_sem.at[2, j]).start()
+            pltpu.make_async_copy(gout.at[:, cols], gh_ref.at[:, cols], out_sem.at[PARTS, j]).start()
 
     opp, own = 1 - w // 2, w // 2
     wait_hidden(0)
@@ -384,49 +396,65 @@
     pair_sum(0)
     xag[1].relay()
     yrs[0].relay()
+    yrs[1].relay()
     z_sum(0)
+    z_sum(1)
     hidden_terms(1)
     z_gather(0)
+    z_gather(1)
     pair_sum(1)
     y_gather(0)
-    head_terms((0, 1))
-    yrs[1].relay()
+    y_gather(1)
+    head_terms((0,))
+    yrs[2].relay()
+    head_terms((1,))
+    yrs[3].relay()
     yag[0].relay()
+    yag[1].relay()
+    z_sum(2)
     head_terms((2,))
-    z_sum(1)
+    z_sum(3)
     put_hidden(0)
-    head_terms((3, 4))
-    z_gather(1)
+    put_hidden(1)
+    head_terms((3,))
+    z_gather(2)
+    head_terms((4,))
+    z_gather(3)
+    y_gather(2)
     head_terms((5,))
-    y_gather(1)
-    head_terms((6, 7))
-    yag[1].relay()
+    y_gather(3)
+    head_terms((6,))
+    yag[2].relay()
+    head_terms((7,))
+    yag[3].relay()
     for k in range(K):
         span3 = divs.at[k, pl.ds(0, 3)]
         remote(span3, span3, DIV, k, x_dev(lax.rem(w + 1, 4))).wait_recv()
         for i in range(2):
             div_ref[2 * k + i : 2 * k + i + 1] = divs[k, 2 * c + i, 0:1]
-    put_hidden(1)
+    put_hidden(2)
+    put_hidden(3)
 
     for k in range(K):
         hid_sends[k].wait_send()
-        for r in (xrs[k], xag[k], yrs[k], yag[k]):
+        for r in (xrs[k], xag[k]):
             r.drain()
         remote(seven(st1, k), seven(st1, k), STAT1, k, cy(1)).wait_send()
         remote(seven(st3, k), seven(st3, k), STAT2, k, z_dev(1)).wait_send()
-        remote(theirs.at[k], arrive.at[k], PAIRSUM, k, partner).wait_send()
-        remote(seven(zin, k), seven(zin, k), ZSUM, k, z_dev(1)).wait_send()
-        span = fin.at[k, y, :, pl.ds(0, 7 * COL8)]
-        remote(span, span, ZOUT, k, z_dev(1)).wait_send()
         span3 = divs.at[k, pl.ds(0, 3)]
         remote(span3, span3, DIV, k, x_dev(lax.rem(w + 1, 4))).wait_send()
+    for n in range(PARTS):
+        for r in (yrs[n], yag[n]):
+            r.drain()
+        remote(theirs.at[n], arrive.at[n], PAIRSUM, n, partner).wait_send()
+        remote(seven(zin, n), seven(zin, n), ZSUM, n, z_dev(1)).wait_send()
+        span = fin.at[n, y, :, pl.ds(0, 7 * COL8)]
+        remote(span, span, ZOUT, n, z_dev(1)).wait_send()
         for i in range(4):
-            pltpu.make_async_copy(
-                fin.at[k, i], ghid_ref.at[pl.ds(k * PAIR + i * TOK4, TOK4)], out_sem.at[k, i]
-            ).wait()
+            out_copy(n, i).wait()
     for j in range(8):
         cols = slice(j * 256, (j + 1) * 256)
-        pltpu.make_async_copy(gout.at[:, cols], gh_ref.at[:, cols], out_sem.at[2, j]).wait()
+        pltpu.make_async_copy(gout.at[:, cols], gh_ref.at[:, cols], out_sem.at[PARTS, j]).wait()
 
     @pl.when(holder)
     def _():
@@ -462,22 +490,22 @@
             vmem((K, 8, 8, BLK), F32),
             vmem((K, 4, ROWS, BLK), BF16),
             vmem((PAIR, ROWS), BF16),
-            vmem((K, PAIR, WID), BF16),
-            vmem((K, PAIR, WID), BF16),
+            vmem((PARTS, PAIR, WID2), BF16),
+            vmem((PARTS, PAIR, WID2), BF16),
             vmem((PAIR, WID), F32),
-            vmem((K, 4, TOK4, WID), BF16),
-            vmem((K, 2, TOK4 // 2, WID), BF16),
-            vmem((K, 2, TOK4, WID), BF16),
-            vmem((K, 8, TOK4, COL8), BF16),
-            vmem((K, 8, TOK4, COL8), BF16),
-            vmem((K, 4, TOK4, WID), BF16),
+            vmem((PARTS, 4, TOK4, WID2), BF16),
+            vmem((PARTS, 2, TOK4 // 2, WID2), BF16),
+            vmem((PARTS, 2, TOK4, WID2), BF16),
+            vmem((PARTS, 8, TOK4, COL8), BF16),
+            vmem((PARTS, 8, TOK4, COL8), BF16),
+            vmem((PARTS, 4, TOK4, WID2), BF16),
             vmem((REAL, WID), BF16),
             vmem((K, 4, 8, BLK), F32),
-            pltpu.SemaphoreType.DMA((K, NSEM)),
-            pltpu.SemaphoreType.DMA((K, NSEM)),
+            pltpu.SemaphoreType.DMA((PARTS, NSEM)),
+            pltpu.SemaphoreType.DMA((PARTS, NSEM)),
             pltpu.SemaphoreType.DMA((K, 2)),
             pltpu.SemaphoreType.DMA((1,)),
-            pltpu.SemaphoreType.DMA((3, 8)),
+            pltpu.SemaphoreType.DMA((PARTS + 1, 8)),
         ],
         compiler_params=pltpu.CompilerParams(
             collective_id=0, has_side_effects=True, vmem_limit_bytes=60 * 1024 * 1024

time: 139 us -> 136 us (0.978)
  Pallas kernels: 128 us -> 125 us
    pallas_call x1, Pallas kernels: 128 us -> 125 us  [body(): pl.pallas_call(kernel, out_shape=(jax.ShapeDtypeStruct((4, BLK), F32), ja...]
where the time goes in v3:
time: 136 us
  Pallas kernels  125 us (92%)
  local copies, waits for them, and re-layouts  10.7 us (8%)
    pallas_call x1, Pallas kernels, body(): pl.pallas_call(kernel, out_shape=(jax.ShapeDtypeStruct((4, BLK), F32), ja...  125 us
    unnamed x6, local copies, waits for them, and re-layouts  10.7 us

profile of v3, /device:TPU:8, one launch (start us, length us, event | category | flops | bytes accessed | tf_op | source)
XLA Modules:
  0.0 136.1 jit_solution(14080094738376071737)
XLA Ops:
  0.6 3.2 %copy.8 = bf16[512,2,1002]{0,2,1:T(8,128)(2,1)} copy(bf16[512,2,1002]{0,1,2:T(2,128)(2,1)} %param.5) | data formatting | bytes 4104192 | tf_op args[2]
  3.8 124.8 %shard_map.58 = (f32[4,128]{1,0:T(4,128)}, bf16[1002,2048]{1,0:T(8,128)(2,1)}, bf16[512,2048]{1,0:T(8,128)(2,1)}) custom-call(bf16[512,2048]{1,0:T(8,128)(2,1)} %hid_ref.1, bf16[1002,2048]{1,0:T(8,128)(2,1)} %bitcast.11, bf16[2,1002,512]{2,1,0:T(8,128)(2,1)} %bitcast.10), custom_call_target="tpu_custom_call" | custom-call | tf_op jit(solution)/shard_map/pallas_call | solution.py:470
  128.6 1.3 copy.12
  129.9 0.0 copy-start
  129.9 4.9 %copy.13 = bf16[2048,1,1002]{0,2,1:T(8,128)(2,1)} copy(bf16[2048,1,1002]{0,2,1:T(8,128)(2,1)} %bitcast.12) | data formatting | bytes 8208384
  134.8 0.0 copy-done
  134.8 1.3 copy.14
Async XLA Ops:
  129.9 4.9 %copy-start = (bf16[512,2048]{1,0:T(8,128)(2,1)S(1)}, bf16[512,2048]{1,0:T(8,128)(2,1)}, u32[]{:S(2)}) copy-start(bf16[512,2048]{1,0:T(8,128)(2,1)} %get-tuple-element.14) | copy-start | bytes 6291460
